TPU v7x, 512 devices: a whole 4x4x16 slice. The times are simulated.
512 devices in a mesh: dp: 2 (over z_hi), fsdp: 16 (over z_lo, core), tile: 16 (over y, x).
Axes of the slice: x: 4, y: 4, z: 16 (z_hi: 2, z_lo: 8; z = z_hi * 8 + z_lo), core: 2. Of those that a mesh axis runs over, the one named last changes fastest.
Arguments:
- tokens: bfloat16 [32, 8, 512, 1536], P(('dp', 'fsdp'), None, 'tile'), may hold values from -6 to 6
- norm_gain: float32 [1536], replicated, may hold values from 0.25 to 1.75
- query_key_value_weight: bfloat16 [1536, 2304], P('fsdp'), may hold values from -5 to 5
- out_weight: bfloat16 [768, 1536], P('fsdp'), may hold values from -0.21875 to 0.21875
- head_weight: bfloat16 [1536, 320], P('fsdp'), may hold values from -0.15625 to 0.15625
- coarse: float32 [32, 20, 8, 512], P(('dp', 'fsdp'), None, None, 'tile'), may hold values from -36 to 36
- grad_fine: float32 [32, 20, 32, 2048], P(('dp', 'fsdp'), None, None, 'tile'), may hold values from -0.6 to 0.6
Outputs:
- fine_grid: float32 [32, 20, 32, 2048], P(('dp', 'fsdp'), None, None, 'tile')
- grad_tokens: bfloat16 [32, 8, 512, 1536], P(('dp', 'fsdp'), None, 'tile')
- grad_head: float32 [1536, 320], P('fsdp')
All inputs are finite; a program needn't handle non-finite values.
Results may differ from a plain program's by a relative error of at most 0.0059.
Values may be sent and summed in bfloat16 or wider, within the bound.
No kernel may reach another device: no remote copies, remote signals or barrier semaphores. Data moves between devices by JAX's collectives and lax.ppermute only.
A program may use at most 64 MiB of HBM per device.

v0:
```python
import jax
import jax.numpy as jnp
from jax import lax
from jax.sharding import PartitionSpec as P

D = 1536
HEADS = 8
HEAD_DIM = 96
VARS = 20
MARGIN = 8
INNER = 768
HEAD_OUT = 320
EPSILON = 1e-05


def with_halo(shard, sides, width):
    for axis, dim in sides:
        devices, length = (lax.axis_size(axis), shard.shape[dim])
        up = [(i, (i + 1) % devices) for i in range(devices)]
        down = [(j, i) for i, j in up]
        last = lax.slice_in_dim(shard, length - width, length, axis=dim)
        leading = lax.slice_in_dim(shard, 0, width, axis=dim)
        before = lax.ppermute(last, axis, up)
        after = lax.ppermute(leading, axis, down)
        shard = jnp.concatenate([before, shard, after], axis=dim)
    return shard


def from_behind(value, axis, steps):
    count = lax.axis_size(axis)
    pairs = [(source, (source + steps) % count) for source in range(count)]
    return lax.ppermute(value, axis, pairs)


def layer_norm(values):
    average = jnp.mean(values, axis=-1, keepdims=True)
    centred = values - average
    variance = jnp.mean(centred * centred, axis=-1, keepdims=True)
    inverse_dev = lax.rsqrt(variance + EPSILON)
    return (centred * inverse_dev, inverse_dev)


def norm_backward(grad_normed, standard, inverse_dev, norm_gain):
    grad_standard = grad_normed * norm_gain
    first_mean = jnp.mean(grad_standard, axis=-1, keepdims=True)
    second_mean = jnp.mean(grad_standard * standard, axis=-1, keepdims=True)
    return inverse_dev * (grad_standard - first_mean - standard * second_mean)


def attend_forward(queries, keys_values):
    query_count = queries.shape[0]
    key_count = keys_values.shape[0]
    score_scale = HEAD_DIM ** (-0.5)
    query_heads = queries.reshape(query_count, HEADS, HEAD_DIM)
    key_heads = keys_values[:, :INNER].reshape(key_count, HEADS, HEAD_DIM)
    value_heads = keys_values[:, INNER:].reshape(key_count, HEADS, HEAD_DIM)
    scores = (
        jnp.einsum("qhd,khd->hqk", query_heads, key_heads, preferred_element_type=jnp.float32)
        * score_scale
    )
    biggest = jnp.max(scores, axis=-1, keepdims=True)
    exponent = jnp.exp(scores - biggest)
    softmax_out = exponent / jnp.sum(exponent, axis=-1, keepdims=True)
    softmax_low = softmax_out.astype(jnp.bfloat16)
    attended = jnp.einsum(
        "hqk,khd->qhd", softmax_low, value_heads, preferred_element_type=jnp.float32
    )
    return (attended.astype(jnp.bfloat16).reshape(query_count, INNER), softmax_out)


def attend_backward(softmax_out, queries, keys_values, grad_attended):
    query_count = queries.shape[0]
    key_count = keys_values.shape[0]
    score_scale = HEAD_DIM ** (-0.5)
    query_heads = queries.reshape(query_count, HEADS, HEAD_DIM)
    key_heads = keys_values[:, :INNER].reshape(key_count, HEADS, HEAD_DIM)
    value_heads = keys_values[:, INNER:].reshape(key_count, HEADS, HEAD_DIM)
    grad_heads = grad_attended.reshape(query_count, HEADS, HEAD_DIM)
    softmax_low = softmax_out.astype(jnp.bfloat16)
    grad_values = jnp.einsum(
        "hqk,qhd->khd", softmax_low, grad_heads, preferred_element_type=jnp.float32
    )
    grad_weights = jnp.einsum(
        "qhd,khd->hqk", grad_heads, value_heads, preferred_element_type=jnp.float32
    )
    weighted = jnp.sum(softmax_out * grad_weights, axis=-1, keepdims=True)
    grad_scores = (softmax_out * (grad_weights - weighted)).astype(jnp.bfloat16)
    grad_queries = (
        jnp.einsum("hqk,khd->qhd", grad_scores, key_heads, preferred_element_type=jnp.float32)
        * score_scale
    )
    grad_keys = (
        jnp.einsum("hqk,qhd->khd", grad_scores, query_heads, preferred_element_type=jnp.float32)
        * score_scale
    )
    pair_gradient_rows = jnp.concatenate(
        [grad_keys.reshape(key_count, INNER), grad_values.reshape(key_count, INNER)], axis=1
    )
    return (grad_queries.astype(jnp.bfloat16).reshape(query_count, INNER), pair_gradient_rows)


def interp_weights(fine_index):
    coarse_cell = fine_index // 4
    phase_index = fine_index % 4
    lower_shift = (phase_index < 2).astype(jnp.int32)
    upper_weight = (2 * phase_index - 3 + 8 * lower_shift).astype(jnp.float32) / 8.0
    return (coarse_cell - lower_shift, upper_weight)


def build_matrix(lower_cell, upper_cell, upper_weight, count):
    columns = jnp.arange(count, dtype=jnp.int32)
    lower_part = jnp.where(
        columns[None, :] == lower_cell[:, None], 1.0 - upper_weight[:, None], 0.0
    )
    upper_portion = jnp.where(columns[None, :] == upper_cell[:, None], upper_weight[:, None], 0.0)
    return lower_part + upper_portion


def contract_last(left_side, right_side):
    return lax.dot_general(
        left_side, right_side, (((1,), (1,)), ((), ())), preferred_element_type=jnp.float32
    )


def shards(tokens, norm_gain, query_key_value_weight, out_weight, head_weight, coarse, grad_fine):
    lat_rows = tokens.shape[1]
    lon_cols = tokens.shape[2]
    row_count = lat_rows * lon_cols
    flattened_rows = tokens[0].reshape(row_count, D).astype(jnp.float32)
    standard, inverse_dev = layer_norm(flattened_rows)
    normed = (standard * norm_gain).astype(jnp.bfloat16)
    full_qkv = lax.all_gather(query_key_value_weight, "fsdp", axis=0, tiled=True)
    projected = jnp.dot(normed, full_qkv, preferred_element_type=jnp.float32).astype(jnp.bfloat16)
    queries = projected[:, :INNER]
    pairs_local = projected[:, INNER:]
    margin_pairs = with_halo(
        pairs_local.reshape(lat_rows, lon_cols, 2 * INNER), (("tile", 1),), MARGIN
    )
    keys_values = margin_pairs.reshape(lat_rows * (lon_cols + 2 * MARGIN), 2 * INNER)
    attended, softmax_out = attend_forward(queries, keys_values)
    full_out = lax.all_gather(out_weight, "fsdp", axis=0, tiled=True)
    mixed_out = jnp.dot(attended, full_out, preferred_element_type=jnp.float32)
    hidden = (flattened_rows + mixed_out).astype(jnp.bfloat16)
    full_head = lax.all_gather(head_weight, "fsdp", axis=0, tiled=True)
    head_out = jnp.dot(hidden, full_head, preferred_element_type=jnp.float32)
    fine_head = (
        head_out.reshape(lat_rows, lon_cols, VARS, 4, 4)
        .transpose(2, 0, 3, 1, 4)
        .reshape(VARS, 4 * lat_rows, 4 * lon_cols)
    )
    coarse_padded_grid = with_halo(coarse[0], (("tile", 2),), 1)
    lat_lower, lat_upper_weight = interp_weights(jnp.arange(4 * lat_rows, dtype=jnp.int32))
    latitude_matrix = build_matrix(
        jnp.clip(lat_lower, 0, lat_rows - 1),
        jnp.clip(lat_lower + 1, 0, lat_rows - 1),
        lat_upper_weight,
        lat_rows,
    )
    lon_lower, lon_upper_weight = interp_weights(jnp.arange(4 * lon_cols, dtype=jnp.int32))
    lon_matrix = build_matrix(lon_lower + 1, lon_lower + 2, lon_upper_weight, lon_cols + 2)
    incomplete_grid = jnp.einsum(
        "lj,kji->kli", latitude_matrix, coarse_padded_grid, precision=lax.Precision.HIGHEST
    )
    residual = jnp.einsum(
        "vrb,cb->vrc", incomplete_grid, lon_matrix, precision=lax.Precision.HIGHEST
    )
    fine_grid = fine_head + residual
    grad_rows = (
        grad_fine[0]
        .reshape(VARS, lat_rows, 4, lon_cols, 4)
        .transpose(1, 3, 0, 2, 4)
        .reshape(row_count, HEAD_OUT)
    )
    grad_rows = grad_rows.astype(jnp.bfloat16)
    head_term = lax.dot_general(
        hidden, grad_rows, (((0,), (0,)), ((), ())), preferred_element_type=jnp.float32
    )
    head_block = lax.psum_scatter(head_term, "fsdp", scatter_dimension=0, tiled=True)
    grad_head = lax.psum(head_block, ("dp", "tile"))
    grad_hidden = contract_last(grad_rows, full_head)
    grad_attended = contract_last(grad_hidden.astype(jnp.bfloat16), full_out).astype(jnp.bfloat16)
    grad_queries, pair_gradient_rows = attend_backward(
        softmax_out, queries, keys_values, grad_attended
    )
    pair_gradient_rows = pair_gradient_rows.reshape(lat_rows, lon_cols + 2 * MARGIN, 2 * INNER)
    from_left = from_behind(pair_gradient_rows[:, lon_cols + MARGIN :], "tile", 1)
    from_right = from_behind(pair_gradient_rows[:, :MARGIN], "tile", -1)
    own_cells = pair_gradient_rows[:, MARGIN : MARGIN + lon_cols]
    own_cells = own_cells + jnp.pad(from_left, ((0, 0), (0, lon_cols - MARGIN), (0, 0)))
    own_cells = own_cells + jnp.pad(from_right, ((0, 0), (lon_cols - MARGIN, 0), (0, 0)))
    grad_all = jnp.concatenate(
        [grad_queries, own_cells.reshape(row_count, 2 * INNER).astype(jnp.bfloat16)], axis=1
    )
    grad_normed = contract_last(grad_all, full_qkv)
    grad_input = grad_hidden + norm_backward(grad_normed, standard, inverse_dev, norm_gain)
    grad_tokens = grad_input.astype(jnp.bfloat16).reshape(1, lat_rows, lon_cols, D)
    return (fine_grid[None], grad_tokens, grad_head)


def solution(mesh):
    placed = (
        P(("dp", "fsdp"), None, "tile", None),
        P(),
        P("fsdp", None),
        P("fsdp", None),
        P("fsdp", None),
        P(("dp", "fsdp"), None, None, "tile"),
        P(("dp", "fsdp"), None, None, "tile"),
    )
    return jax.shard_map(
        shards,
        mesh=mesh,
        in_specs=placed,
        out_specs=(
            P(("dp", "fsdp"), None, None, "tile"),
            P(("dp", "fsdp"), None, "tile", None),
            P("fsdp", None),
        ),
        check_vma=False,
    )
```

profile of v0, /device:TPU:2, one launch (start us, length us, event | category | flops | bytes accessed | tf_op | source)
XLA Modules:
  0.0 943.6 jit_solution(4857148850893295786)
XLA Ops:
  10.4 3.4 collective-permute-start.2
  13.8 6.3 collective-permute-start.3
  25.7 46.6 %all_gather.11 = bf16[1536,320]{1,0:T(8,128)(2,1)S(1)} all-gather(bf16[96,320]{1,0:T(8,128)(2,1)} %param.11), channel_id=1, replica_groups=mesh['dp'=2,'fsdp'=16,'tile'=16] {'fsdp'}, dimensions={0}, use_global_device_ids=true | all-gather | bytes 1044480 | tf_op jit(solution)/shard_map/all_gather | solution.py:144
  75.7 2.1 convolution_bitcast_fusion.1
  77.8 55.1 %all-gather.3.cloned.1.call-done = bf16[1536,2304]{1,0:T(8,128)(2,1)} async-done(((bf16[96,2304]{1,0:T(8,128)(2,1)}), bf16[1536,2304]{1,0:T(8,128)(2,1)}) %all-gather.3.cloned.1.call-update) | async-done | bytes 7077904 | tf_op jit(solution)/shard_map/all_gather | solution.py:132
  132.9 5.3 convolution_convert_fusion
  140.0 3.2 collective-permute-start
  143.2 2.8 collective-permute-start.1
  146.0 86.6 %all-gather.5.cloned.1.call-done = bf16[768,1536]{1,0:T(8,128)(2,1)} async-done(((bf16[48,1536]{1,0:T(8,128)(2,1)}), bf16[768,1536]{1,0:T(8,128)(2,1)}) %all-gather.5.cloned.1.call-update) | async-done | bytes 2359312 | tf_op jit(solution)/shard_map/all_gather | solution.py:141
  232.6 3.2 convolution_convert_fusion.1
  235.8 1.9 copy.24
  237.8 1.8 slice.50
  239.6 1.9 copy.18
  243.9 2.1 copy.29
  246.1 2.1 copy.28
  248.2 4.0 fusion.57
  252.2 2.9 convolution_convert_fusion.2
  257.3 2.0 fusion.60
  260.7 3.0 copy.20
  263.8 3.0 copy.21
  266.8 2.6 convolution_bitcast_fusion
  271.0 2.7 concatenate.20
  274.9 3.0 multiply_reduce_fusion
  281.9 1.9 concatenate.19
  287.6 3.4 collective-permute-start.4
  291.1 2.8 collective-permute-start.5
  296.7 3.5 collective-permute-done.4
  300.2 3.3 collective-permute-done.5
  305.2 6.3 fusion.52
  311.6 73.0 %reduce-scatter.2.cloned.1.call-done = f32[96,320]{1,0:T(8,128)} async-done(((f32[1536,320]{1,0:T(8,128)}), f32[96,320]{1,0:T(8,128)}) %reduce-scatter.2.cloned.1.call-update) | async-done | bytes 122896 | tf_op jit(solution)/shard_map/reduce_scatter | solution.py:178
  384.5 2.9 add_convert_fusion
  387.4 548.1 %all-reduce.4.cloned.1.call-done = f32[96,320]{1,0:T(8,128)} async-done(((f32[96,320]{1,0:T(8,128)}), f32[96,320]{1,0:T(8,128)}) %all-reduce.4.cloned.1.call-update) | async-done | bytes 122896 | tf_op jit(solution)/shard_map/psum | solution.py:179
  (101 shorter events, 36.6 us)
Async XLA Ops:
  7.2 14.4 %copy-start = (bf16[1,8,32,1536]{3,2,1,0:T(8,128)(2,1)S(1)}, bf16[1,8,32,1536]{3,2,1,0:T(8,128)(2,1)}, u32[]{:S(2)}) copy-start(bf16[1,8,32,1536]{3,2,1,0:T(8,128)(2,1)} %param.7) | copy-start | bytes 2359300
  7.2 14.8 %copy-start.19 = (f32[1,20,32,128]{3,2,1,0:T(8,128)S(1)}, f32[1,20,32,128]{3,2,1,0:T(8,128)}, u32[]{:S(2)}) copy-start(f32[1,20,32,128]{3,2,1,0:T(8,128)} %param.13) | copy-start | bytes 983044
  7.2 125.7 %all-gather.3.cloned.1.call-start = ((), (), s32[]{:S(2)}) async-start(), calls=%async_computation.1 | async-start | bytes 7520256 | tf_op jit(solution)/shard_map/all_gather | solution.py:132
  7.9 224.7 %all-gather.5.cloned.1.call-start = ((), (), s32[]{:S(2)}) async-start(), calls=%async_computation.2 | async-start | bytes 2506752 | tf_op jit(solution)/shard_map/all_gather | solution.py:141
  8.7 375.8 %reduce-scatter.2.cloned.1.call-start = ((), (), s32[]{:S(2)}) async-start(), calls=%async_computation.3 | async-start | bytes 2506752 | tf_op jit(solution)/shard_map/reduce_scatter | solution.py:178
  10.4 65.2 %collective-permute-start.2 = (f32[20,8,1]{2,1,0:T(8,128)}, f32[20,8,1]{2,1,0:T(8,128)}, u32[]{:S(2)}, u32[]{:S(2)}) collective-permute-start(f32[20,8,1]{2,1,0:T(8,128)} %get-tuple-element.11), channel_id=1, source_target_pairs={{0,1},{1,2},{2,3},{3,4},{4,5},{5,6},{6,7},{7,8},{8,9},{9,10},{10,1... | collective-permute-start | bytes 1928 | tf_op jit(solution)/shard_map/ppermute | solution.py:23
  13.8 61.8 %collective-permute-start.3 = (f32[20,8,1]{2,1,0:T(8,128)}, f32[20,8,1]{2,1,0:T(8,128)}, u32[]{:S(2)}, u32[]{:S(2)}) collective-permute-start(f32[20,8,1]{2,1,0:T(8,128)} %get-tuple-element.12), channel_id=1, source_target_pairs={{1,0},{2,1},{3,2},{4,3},{5,4},{6,5},{7,6},{8,7},{9,8},{10,9},{11,1... | collective-permute-start | bytes 1928 | tf_op jit(solution)/shard_map/ppermute | solution.py:24
  72.3 1.6 copy-start.20
  72.3 3.4 copy-start.15
  138.2 1.8 copy-start.14
  140.0 101.5 %collective-permute-start = (bf16[8,8,1536]{2,1,0:T(8,128)(2,1)}, bf16[8,8,1536]{2,1,0:T(8,128)(2,1)}, u32[]{:S(2)}, u32[]{:S(2)}) collective-permute-start(bf16[8,8,1536]{2,1,0:T(8,128)(2,1)} %get-tuple-element.9), channel_id=1, source_target_pairs={{0,1},{1,2},{2,3},{3,4},{4,5},{5,6},{6,7},{7,8},{8,9},{9,10},{10,1... | collective-permute-start | bytes 589832 | tf_op jit(solution)/shard_map/ppermute | solution.py:23
  143.2 98.3 %collective-permute-start.1 = (bf16[8,8,1536]{2,1,0:T(8,128)(2,1)}, bf16[8,8,1536]{2,1,0:T(8,128)(2,1)}, u32[]{:S(2)}, u32[]{:S(2)}) collective-permute-start(bf16[8,8,1536]{2,1,0:T(8,128)(2,1)} %get-tuple-element.10), channel_id=1, source_target_pairs={{1,0},{2,1},{3,2},{4,3},{5,4},{6,5},{7,6},{8,7},{9,8},{10,9},{11,1... | collective-permute-start | bytes 589832 | tf_op jit(solution)/shard_map/ppermute | solution.py:24
  252.2 2.9 copy-start.4
  256.0 1.3 copy-start.10
  257.3 2.0 copy-start.12
  273.7 661.8 %all-reduce.4.cloned.1.call-start = ((), (), s32[]{:S(2)}) async-start(), calls=%async_computation.4 | async-start | bytes 294912 | tf_op jit(solution)/shard_map/psum | solution.py:179
  274.9 3.0 copy-start.3
  277.9 1.9 copy-start.9
  283.8 1.3 copy-start.8
  285.0 8.9 copy-start.2
  285.0 8.9 copy-start.6
  285.2 1.5 copy-start.5
  287.6 12.6 %collective-permute-start.4 = (f32[8,8,1536]{2,1,0:T(8,128)}, f32[8,8,1536]{2,1,0:T(8,128)}, u32[]{:S(2)}, u32[]{:S(2)}) collective-permute-start(f32[8,8,1536]{2,1,0:T(8,128)} %get-tuple-element.5), channel_id=1, source_target_pairs={{0,1},{1,2},{2,3},{3,4},{4,5},{5,6},{6,7},{7,8},{8,9},{9,10},{10,1... | collective-permute-start | bytes 1179656 | tf_op jit(solution)/shard_map/ppermute | solution.py:32
  291.0 4.5 copy-start.11
  291.0 4.5 copy-start.13
  291.0 4.5 copy-start.22
  291.0 4.5 copy-start.23
  291.0 4.5 copy-start.24
  291.1 4.5 copy-start.25
  291.1 12.4 %collective-permute-start.5 = (f32[8,8,1536]{2,1,0:T(8,128)}, f32[8,8,1536]{2,1,0:T(8,128)}, u32[]{:S(2)}, u32[]{:S(2)}) collective-permute-start(f32[8,8,1536]{2,1,0:T(8,128)} %get-tuple-element.6), channel_id=1, source_target_pairs={{0,15},{1,0},{2,1},{3,2},{4,3},{5,4},{6,5},{7,6},{8,7},{9,8},{10,9... | collective-permute-start | bytes 1179656 | tf_op jit(solution)/shard_map/ppermute | solution.py:32
  296.7 8.5 copy-start.18
  296.7 8.6 copy-start.21
  (4 other events, 4.4 us)
Sparse Core Ops, SparseCore 0:
  10.1 122.7 all-gather.2
  135.0 97.5 all-gather.4
  273.8 110.6 reduce-scatter.1
  387.3 548.2 all-reduce.3
where the time goes:
time: 945 us; the launch traced here: 944 us
  waiting for transfers between devices  771 us (82%)
  blocking collectives  46.6 us (5%)
  local copies, waits for them, and re-layouts  41.8 us (4%)
  matrix products  37.3 us (4%)
  starting transfers between devices  22.1 us (2%)
  between operations  14.2 us (2%)
  other arithmetic  10.8 us (1%)
    psum x1, waiting for transfers between devices, shards(): grad_head = lax.psum(head_block, ('dp', 'tile'))  548 us
    all_gather x1, waiting for transfers between devices, shards(): full_out = lax.all_gather(out_weight, 'fsdp', axis=0, tiled=True)  86.6 us
    reduce_scatter x1, waiting for transfers between devices, shards(): lax.psum_scatter(head_term, 'fsdp', scatter_dimension=0, tiled=True)  73 us
    all_gather x1, waiting for transfers between devices, shards(): lax.all_gather(query_key_value_weight, 'fsdp', axis=0, tiled=True)  55.1 us
    all_gather x1, blocking collectives, shards(): full_head = lax.all_gather(head_weight, 'fsdp', axis=0, tiled=True)  46.6 us
  transfers between devices with their start and end apart: 10, of which 6 were waited for; matrix products, arithmetic and copies ran while one was open for 5% of the time, Pallas kernels for 0%

commit v1 on v0

--- a/solution.py
+++ b/solution.py
@@ -176,7 +176,7 @@
         hidden, grad_rows, (((0,), (0,)), ((), ())), preferred_element_type=jnp.float32
     )
     head_block = lax.psum_scatter(head_term, "fsdp", scatter_dimension=0, tiled=True)
-    grad_head = lax.psum(head_block, ("dp", "tile"))
+    grad_head = lax.psum(lax.psum(head_block, "tile"), "dp")
     grad_hidden = contract_last(grad_rows, full_head)
     grad_attended = contract_last(grad_hidden.astype(jnp.bfloat16), full_out).astype(jnp.bfloat16)
     grad_queries, pair_gradient_rows = attend_backward(

time: 945 us -> 557 us (0.59)
  the two profiles are of different devices: /device:TPU:2 before, /device:TPU:1 now
where the time goes in v1:
time: 557 us; the launch traced here: 556 us
  waiting for transfers between devices  371 us (67%)
  blocking collectives  50 us (9%)
  local copies, waits for them, and re-layouts  43.4 us (8%)
  matrix products  39.1 us (7%)
  starting transfers between devices  27.1 us (5%)
  between operations  14.1 us (3%)
  other arithmetic  11.4 us (2%)
    psum x2, waiting for transfers between devices, shards(): grad_head = lax.psum(lax.psum(head_block, 'tile'), 'dp')  178 us
    all_gather x1, waiting for transfers between devices, shards(): full_out = lax.all_gather(out_weight, 'fsdp', axis=0, tiled=True)  87 us
    reduce_scatter x1, waiting for transfers between devices, shards(): lax.psum_scatter(head_term, 'fsdp', scatter_dimension=0, tiled=True)  52.7 us
    all_gather x1, blocking collectives, shards(): full_head = lax.all_gather(head_weight, 'fsdp', axis=0, tiled=True)  50 us
    all_gather x1, waiting for transfers between devices, shards(): lax.all_gather(query_key_value_weight, 'fsdp', axis=0, tiled=True)  49 us
    unnamed x58, local copies, waits for them, and re-layouts  12.2 us
    ppermute x2, starting transfers between devices, with_halo(): after = lax.ppermute(leading, axis, down)  11.8 us
    dot_general x3, matrix products, contract_last(): lax.dot_general(left_side, right_side, (((1,), (1,)), ((), ())), preferre...  11.7 us
  transfers between devices with their start and end apart: 11, of which 7 were waited for; matrix products, arithmetic and copies ran while one was open for 12% of the time, Pallas kernels for 0%

profile of v1, /device:TPU:1, one launch (start us, length us, event | category | flops | bytes accessed | tf_op | source)
XLA Modules:
  0.0 555.7 jit_solution(5916759297751713066)
XLA Ops:
  10.4 3.9 collective-permute-start.2
  14.3 5.6 %collective-permute-start.3 = (f32[20,8,1]{2,1,0:T(8,128)}, f32[20,8,1]{2,1,0:T(8,128)}, u32[]{:S(2)}, u32[]{:S(2)}) collective-permute-start(f32[20,8,1]{2,1,0:T(8,128)} %get-tuple-element.12), channel_id=1, source_target_pairs={{1,0},{2,1},{3,2},{4,3},{5,4},{6,5},{7,6},{8,7},{9,8},{10,9},{11,1... | collective-permute-start | bytes 1928 | tf_op jit(solution)/shard_map/ppermute | solution.py:24
  25.6 50.0 %all_gather.11 = bf16[1536,320]{1,0:T(8,128)(2,1)S(1)} all-gather(bf16[96,320]{1,0:T(8,128)(2,1)} %param.11), channel_id=1, replica_groups=mesh['dp'=2,'fsdp'=16,'tile'=16] {'fsdp'}, dimensions={0}, use_global_device_ids=true | all-gather | bytes 1044480 | tf_op jit(solution)/shard_map/all_gather | solution.py:144
  78.9 2.1 convolution_bitcast_fusion.1
  81.1 49.0 %all-gather.3.cloned.1.call-done = bf16[1536,2304]{1,0:T(8,128)(2,1)} async-done(((bf16[96,2304]{1,0:T(8,128)(2,1)}), bf16[1536,2304]{1,0:T(8,128)(2,1)}) %all-gather.3.cloned.1.call-update) | async-done | bytes 7077904 | tf_op jit(solution)/shard_map/all_gather | solution.py:132
  130.1 5.3 convolution_convert_fusion
  137.1 2.5 collective-permute-start
  139.6 6.1 %collective-permute-start.1 = (bf16[8,8,1536]{2,1,0:T(8,128)(2,1)}, bf16[8,8,1536]{2,1,0:T(8,128)(2,1)}, u32[]{:S(2)}, u32[]{:S(2)}) collective-permute-start(bf16[8,8,1536]{2,1,0:T(8,128)(2,1)} %get-tuple-element.10), channel_id=1, source_target_pairs={{1,0},{2,1},{3,2},{4,3},{5,4},{6,5},{7,6},{8,7},{9,8},{10,9},{11,1... | collective-permute-start | bytes 589832 | tf_op jit(solution)/shard_map/ppermute | solution.py:24
  145.8 87.0 %all-gather.5.cloned.1.call-done = bf16[768,1536]{1,0:T(8,128)(2,1)} async-done(((bf16[48,1536]{1,0:T(8,128)(2,1)}), bf16[768,1536]{1,0:T(8,128)(2,1)}) %all-gather.5.cloned.1.call-update) | async-done | bytes 2359312 | tf_op jit(solution)/shard_map/all_gather | solution.py:141
  232.8 3.2 convolution_convert_fusion.1
  236.0 1.9 copy.24
  239.8 1.9 copy.18
  244.2 2.1 copy.29
  246.3 2.2 copy.28
  248.5 4.0 fusion.57
  252.5 2.9 convolution_convert_fusion.2
  259.3 2.1 fusion.60
  261.6 2.4 fusion.58
  264.0 2.4 reshape.187
  266.4 3.1 copy.20
  269.4 3.1 copy.21
  274.2 2.8 concatenate.20
  277.0 3.0 multiply_reduce_fusion
  284.0 1.9 concatenate.19
  289.7 3.3 collective-permute-start.4
  293.0 5.3 collective-permute-start.5
  300.0 2.2 fusion.11
  306.1 6.9 %fusion.52 = (f32[256]{0:T(256)}, f32[256]{0:T(256)}, f32[256,1536]{1,0:T(8,128)}) fusion(f32[256]{0:T(256)S(1)} %rsqrt.12, f32[256]{0:T(256)S(1)} %div.51, bf16[1,8,32,1536]{3,2,1,0:T(8,128)(2,1)S(1)} %copy-done, f32[1536]{0:T(1024)S(1)} %copy-done.22, bf16[1536,2304]{1,0:T(8,128)(2,1)} %all-gather.3.cloned.1.call-done, ...), kind=kOutput, calls=%fused_computation.104 | convolution fusion | flops 1817050624 | bytes 10627072 | tf_op jit(solution)/shard_map/dot_general | solution.py:120
  313.0 52.7 %reduce-scatter.2.cloned.1.call-done = f32[96,320]{1,0:T(8,128)} async-done(((f32[1536,320]{1,0:T(8,128)}), f32[96,320]{1,0:T(8,128)}) %reduce-scatter.2.cloned.1.call-update) | async-done | bytes 122896 | tf_op jit(solution)/shard_map/reduce_scatter | solution.py:178
  366.4 117.0 %all-reduce.5.cloned.1.call-done = f32[96,320]{1,0:T(8,128)} async-done(((f32[96,320]{1,0:T(8,128)}), f32[96,320]{1,0:T(8,128)}) %all-reduce.5.cloned.1.call-update) | async-done | bytes 122896 | tf_op jit(solution)/shard_map/psum | solution.py:179
  483.4 2.9 add_convert_fusion
  486.3 61.3 %all-reduce.7.cloned.1.call-done = f32[96,320]{1,0:T(8,128)} async-done(((f32[96,320]{1,0:T(8,128)}), f32[96,320]{1,0:T(8,128)}) %all-reduce.7.cloned.1.call-update) | async-done | bytes 122896 | tf_op jit(solution)/shard_map/psum | solution.py:179
  (106 shorter events, 39.5 us)
Async XLA Ops:
  7.2 14.2 %copy-start = (bf16[1,8,32,1536]{3,2,1,0:T(8,128)(2,1)S(1)}, bf16[1,8,32,1536]{3,2,1,0:T(8,128)(2,1)}, u32[]{:S(2)}) copy-start(bf16[1,8,32,1536]{3,2,1,0:T(8,128)(2,1)} %param.7) | copy-start | bytes 2359300
  7.2 14.7 %copy-start.20 = (f32[1,20,32,128]{3,2,1,0:T(8,128)S(1)}, f32[1,20,32,128]{3,2,1,0:T(8,128)}, u32[]{:S(2)}) copy-start(f32[1,20,32,128]{3,2,1,0:T(8,128)} %param.13) | copy-start | bytes 983044
  7.2 122.9 %all-gather.3.cloned.1.call-start = ((), (), s32[]{:S(2)}) async-start(), calls=%async_computation.1 | async-start | bytes 7520256 | tf_op jit(solution)/shard_map/all_gather | solution.py:132
  7.9 224.9 %all-gather.5.cloned.1.call-start = ((), (), s32[]{:S(2)}) async-start(), calls=%async_computation.2 | async-start | bytes 2506752 | tf_op jit(solution)/shard_map/all_gather | solution.py:141
  8.7 357.0 %reduce-scatter.2.cloned.1.call-start = ((), (), s32[]{:S(2)}) async-start(), calls=%async_computation.3 | async-start | bytes 2506752 | tf_op jit(solution)/shard_map/reduce_scatter | solution.py:178
  10.4 68.5 %collective-permute-start.2 = (f32[20,8,1]{2,1,0:T(8,128)}, f32[20,8,1]{2,1,0:T(8,128)}, u32[]{:S(2)}, u32[]{:S(2)}) collective-permute-start(f32[20,8,1]{2,1,0:T(8,128)} %get-tuple-element.11), channel_id=1, source_target_pairs={{0,1},{1,2},{2,3},{3,4},{4,5},{5,6},{6,7},{7,8},{8,9},{9,10},{10,1... | collective-permute-start | bytes 1928 | tf_op jit(solution)/shard_map/ppermute | solution.py:23
  14.3 64.6 %collective-permute-start.3 = (f32[20,8,1]{2,1,0:T(8,128)}, f32[20,8,1]{2,1,0:T(8,128)}, u32[]{:S(2)}, u32[]{:S(2)}) collective-permute-start(f32[20,8,1]{2,1,0:T(8,128)} %get-tuple-element.12), channel_id=1, source_target_pairs={{1,0},{2,1},{3,2},{4,3},{5,4},{6,5},{7,6},{8,7},{9,8},{10,9},{11,1... | collective-permute-start | bytes 1928 | tf_op jit(solution)/shard_map/ppermute | solution.py:24
  75.6 3.4 copy-start.15
  135.3 1.8 copy-start.13
  137.1 104.6 %collective-permute-start = (bf16[8,8,1536]{2,1,0:T(8,128)(2,1)}, bf16[8,8,1536]{2,1,0:T(8,128)(2,1)}, u32[]{:S(2)}, u32[]{:S(2)}) collective-permute-start(bf16[8,8,1536]{2,1,0:T(8,128)(2,1)} %get-tuple-element.9), channel_id=1, source_target_pairs={{0,1},{1,2},{2,3},{3,4},{4,5},{5,6},{6,7},{7,8},{8,9},{9,10},{10,1... | collective-permute-start | bytes 589832 | tf_op jit(solution)/shard_map/ppermute | solution.py:23
  139.6 102.1 %collective-permute-start.1 = (bf16[8,8,1536]{2,1,0:T(8,128)(2,1)}, bf16[8,8,1536]{2,1,0:T(8,128)(2,1)}, u32[]{:S(2)}, u32[]{:S(2)}) collective-permute-start(bf16[8,8,1536]{2,1,0:T(8,128)(2,1)} %get-tuple-element.10), channel_id=1, source_target_pairs={{1,0},{2,1},{3,2},{4,3},{5,4},{6,5},{7,6},{8,7},{9,8},{10,9},{11,1... | collective-permute-start | bytes 589832 | tf_op jit(solution)/shard_map/ppermute | solution.py:24
  252.5 3.0 copy-start.3
  252.5 3.1 copy-start.17
  255.6 2.0 copy-start.5
  257.6 1.7 copy-start.12
  261.3 222.1 %all-reduce.5.cloned.1.call-start = ((), (), s32[]{:S(2)}) async-start(), calls=%async_computation.4 | async-start | bytes 294912 | tf_op jit(solution)/shard_map/psum | solution.py:179
  269.4 3.1 copy-start.14
  274.2 2.8 copy-start.16
  274.2 2.8 copy-start.18
  277.0 3.0 copy-start.4
  279.9 1.9 copy-start.11
  287.1 11.2 %copy-start.2 = (bf16[8,256,384]{2,1,0:T(8,128)(2,1)S(1)}, bf16[8,256,384]{2,1,0:T(8,128)(2,1)}, u32[]{:S(2)}) copy-start(bf16[8,256,384]{2,1,0:T(8,128)(2,1)} %copy-done.1) | copy-start | bytes 4718596
  287.1 11.3 %copy-start.8 = (bf16[384,768]{0,1:T(8,128)(2,1)S(1)}, bf16[384,768]{0,1:T(8,128)(2,1)}, u32[]{:S(2)}) copy-start(bf16[384,768]{0,1:T(8,128)(2,1)} %copy.29) | copy-start | bytes 1769476
  289.7 13.6 %collective-permute-start.4 = (f32[8,8,1536]{2,1,0:T(8,128)}, f32[8,8,1536]{2,1,0:T(8,128)}, u32[]{:S(2)}, u32[]{:S(2)}) collective-permute-start(f32[8,8,1536]{2,1,0:T(8,128)} %get-tuple-element.5), channel_id=1, source_target_pairs={{0,1},{1,2},{2,3},{3,4},{4,5},{5,6},{6,7},{7,8},{8,9},{9,10},{10,1... | collective-permute-start | bytes 1179656 | tf_op jit(solution)/shard_map/ppermute | solution.py:32
  293.0 7.0 %copy-start.23 = (s32[128]{0:T(128)S(1)}, s32[128]{0:T(128)}, u32[]{:S(2)}) copy-start(s32[128]{0:T(128)} %get-tuple-element.24) | copy-start | bytes 1540
  293.0 7.0 %copy-start.24 = (s32[128]{0:T(128)S(1)}, s32[128]{0:T(128)}, u32[]{:S(2)}) copy-start(s32[128]{0:T(128)} %get-tuple-element.25) | copy-start | bytes 1540
  293.0 7.0 %copy-start.25 = (f32[128]{0:T(128)S(1)}, f32[128]{0:T(128)}, u32[]{:S(2)}) copy-start(f32[128]{0:T(128)} %get-tuple-element.22) | copy-start | bytes 1540
  293.0 7.0 %copy-start.26 = (f32[128]{0:T(128)S(1)}, f32[128]{0:T(128)}, u32[]{:S(2)}) copy-start(f32[128]{0:T(128)} %get-tuple-element.23) | copy-start | bytes 1540
  293.0 11.3 %collective-permute-start.5 = (f32[8,8,1536]{2,1,0:T(8,128)}, f32[8,8,1536]{2,1,0:T(8,128)}, u32[]{:S(2)}, u32[]{:S(2)}) collective-permute-start(f32[8,8,1536]{2,1,0:T(8,128)} %get-tuple-element.6), channel_id=1, source_target_pairs={{0,15},{1,0},{2,1},{3,2},{4,3},{5,4},{6,5},{7,6},{8,7},{9,8},{10,9... | collective-permute-start | bytes 1179656 | tf_op jit(solution)/shard_map/ppermute | solution.py:32
  302.2 3.8 copy-start.19
  302.2 3.9 copy-start.22
  365.7 181.9 %all-reduce.7.cloned.1.call-start = ((), (), s32[]{:S(2)}) async-start(), calls=%async_computation.5 | async-start | bytes 294912 | tf_op jit(solution)/shard_map/psum | solution.py:179
  (6 other events, 7.3 us)
Sparse Core Ops, SparseCore 0:
  10.1 119.9 all-gather.2
  132.1 100.6 all-gather.4
  261.5 104.1 reduce-scatter.1
  368.7 114.6 all-reduce.4
  486.1 61.4 all-reduce.6
